TPU v7x, 512 devices: a whole 4x4x16 slice. The times are simulated.
512 devices in a mesh: gz: 16 (over y, x), pa: 32 (over z, core).
Axes of the slice: x: 4, y: 4, z: 16, core: 2. Of those that a mesh axis runs over, the one named last changes fastest.
Arguments:
- particles: float32 [6, 1048576], P(None, ('gz', 'pa')), may hold values from -6 to 6
- slice_index: int32 [1048576], P(('gz', 'pa')), may hold values from 0 to 127
- moving: int32 [16, 32, 2], P('gz', 'pa'), may hold values from 0 to 384, as said below
- decay_rate: float32 [8], replicated, may hold values from 0.3 to 600
- wake_freq: float32 [8], replicated, may hold values from -3.140625 to 3.140625
- wake_amp: float32 [4, 8], replicated, may hold values from -3 to 3
Outputs:
- wake_kick: float32 [3, 2048], P(None, 'gz')
- particles_out: float32 [6, 1441792], P(None, ('gz', 'pa'))
Inputs may be any that keep to these rules, and one draw needn't show every extreme that they name: `moving`: each entry is at most 384, and some entry equals 384.
All inputs are finite; a program needn't handle non-finite values.
Results may differ from a plain program's by a relative error of at most 0.0003.
Values sent between devices are 32-bit elements; how exact they have to be, the bound alone decides.
No kernel may reach another device: no remote copies, remote signals or barrier semaphores. Data moves between devices by JAX's collectives and lax.ppermute only.
A program may use at most 64 MiB of HBM per device.

v0:
```python
import math
import jax
import jax.numpy as jnp
from jax import lax
from jax.sharding import PartitionSpec as P

S_DEV = 128
two_pi = 6.283185307179586
adjust_horiz = 0.269
adjust_vert = 0.355
chroma_horiz = 0.05
chroma_vert = 0.04
curve_horiz = 0.02
curve_vert = -0.015
detune_self = 0.03
detune_cross = -0.02
voltage = 0.05
synch_phase = 0.3
slippage = 0.1


def from_behind_2(value, axis, steps):
    count = lax.axis_size(axis)
    leading, last = (max(0, -steps), min(count, count - steps))
    return lax.ppermute(value, axis, [(source, source + steps) for source in range(leading, last)])


def complex_mul(first, second):
    return jnp.stack(
        [first[0] * second[0] - first[1] * second[1], first[0] * second[1] + first[1] * second[0]]
    )


def powers(damping, wake_freq, distance):
    envelope = jnp.exp(-damping[:, None] * distance[None, :])
    angles = wake_freq[:, None] * distance[None, :]
    return (envelope * jnp.cos(angles), envelope * jnp.sin(angles))


def toeplitz(wave):
    slab_width = wave.shape[0]
    row_index = lax.broadcasted_iota(jnp.int32, (slab_width, slab_width), 0)
    col_index = lax.broadcasted_iota(jnp.int32, (slab_width, slab_width), 1)
    offset = col_index - row_index
    picked = jnp.take(wave, jnp.clip(offset, 0, slab_width - 1))
    return jnp.where(offset > 0, picked, jnp.float32(0.0))


def slab_tables(decay_rate, wake_freq, wake_amp, slab_width, slice_total):
    damping = decay_rate / slice_total
    norm_trans = jnp.sqrt(2.0 * damping)
    norm_long = jnp.sqrt(damping * damping + wake_freq * wake_freq)
    coef_real = jnp.stack(
        [wake_amp[0] * norm_trans, wake_amp[0] * norm_trans, wake_amp[2] * norm_long], axis=1
    )
    coef_imag = jnp.stack(
        [wake_amp[1] * norm_trans, wake_amp[1] * norm_trans, wake_amp[3] * norm_long], axis=1
    )
    distance = jnp.arange(slab_width, dtype=jnp.float32)
    near_re, near_im = powers(damping, wake_freq, distance)
    far_re, far_im = powers(damping, wake_freq, slab_width - distance)
    whole_re, whole_im = powers(damping, wake_freq, jnp.full((1,), slab_width, jnp.float32))
    factor = jnp.stack(
        [jnp.broadcast_to(whole_re, coef_real.shape), jnp.broadcast_to(whole_im, coef_real.shape)]
    )
    wave_trans = jnp.sum(
        norm_trans[:, None] * (wake_amp[0][:, None] * near_re - wake_amp[1][:, None] * near_im),
        axis=0,
    )
    wave_long = jnp.sum(
        norm_long[:, None] * (wake_amp[2][:, None] * near_re - wake_amp[3][:, None] * near_im),
        axis=0,
    )
    return (
        toeplitz(wave_trans),
        toeplitz(wave_long),
        near_re,
        near_im,
        far_re,
        far_im,
        factor,
        coef_real,
        coef_imag,
    )


def slab_summary(moments, tables):
    highest = lax.Precision.HIGHEST
    return jnp.stack(
        [
            jnp.dot(tables[4], moments.T, precision=highest),
            jnp.dot(tables[5], moments.T, precision=highest),
        ]
    )


def slab_kick(moments, carried, tables):
    highest = lax.Precision.HIGHEST
    trans_kick = jnp.dot(moments[0:2], tables[0], precision=highest)
    long_kick = jnp.dot(moments[2:3], tables[1], precision=highest)
    coef_re = tables[7] * carried[0] - tables[8] * carried[1]
    coef_im = tables[7] * carried[1] + tables[8] * carried[0]
    incoming = jnp.dot(coef_re.T, tables[2], precision=highest) - jnp.dot(
        coef_im.T, tables[3], precision=highest
    )
    return jnp.concatenate([trans_kick, long_kick], axis=0) + incoming


def moment_values(particles, mean_fill):
    root_fill = math.sqrt(mean_fill)
    return jnp.stack(
        [
            particles[0] / root_fill,
            particles[2] / root_fill,
            jnp.full_like(particles[0], 1.0 / mean_fill),
        ]
    )


def deposit(values, index, segments):
    return jax.vmap(lambda column: jax.ops.segment_sum(column, index, num_segments=segments))(
        values
    )


def one_turn(coords, kicks):
    hor_pos = coords[0]
    hor_mom = coords[1] + kicks[0]
    ver_pos = coords[2]
    ver_mom = coords[3] + kicks[1]
    lag_pos = coords[4]
    energy_dev = coords[5] + kicks[2]
    action_x = 0.5 * (hor_pos * hor_pos + hor_mom * hor_mom)
    action_y = 0.5 * (ver_pos * ver_pos + ver_mom * ver_mom)
    phase_x = two_pi * (
        adjust_horiz
        + chroma_horiz * energy_dev
        + curve_horiz * energy_dev * energy_dev
        + detune_self * action_x
        + detune_cross * action_y
    )
    phase_y = two_pi * (
        adjust_vert
        + chroma_vert * energy_dev
        + curve_vert * energy_dev * energy_dev
        + detune_self * action_y
        + detune_cross * action_x
    )
    cosine_x = jnp.cos(phase_x)
    sine_x = jnp.sin(phase_x)
    cosine_y = jnp.cos(phase_y)
    sine_y = jnp.sin(phase_y)
    new_energy = energy_dev - voltage * (jnp.sin(synch_phase + lag_pos) - math.sin(synch_phase))
    new_lag = lag_pos - slippage * new_energy
    return jnp.stack(
        [
            cosine_x * hor_pos + sine_x * hor_mom,
            cosine_x * hor_mom - sine_x * hor_pos,
            cosine_y * ver_pos + sine_y * ver_mom,
            cosine_y * ver_mom - sine_y * ver_pos,
            new_lag,
            new_energy,
        ]
    )


def upstream(own_summary, factor, slab_count):

    def advance(step_index, carried):
        return from_behind_2(complex_mul(factor, carried) + own_summary, "gz", 1)

    return lax.fori_loop(0, slab_count - 1, advance, jnp.zeros_like(own_summary))


def body(particles, slice_index, moving, decay_rate, wake_freq, wake_amp):
    slab_count = lax.axis_size("gz")
    member_count = lax.axis_size("pa")
    local_count = particles.shape[1]
    slab_width = S_DEV
    tables = slab_tables(decay_rate, wake_freq, wake_amp, slab_width, slab_width * slab_count)
    mean_fill = local_count * member_count / slab_width
    values = moment_values(particles, mean_fill)
    partial_moments = deposit(values, slice_index, slab_width)
    moments = lax.psum(partial_moments, "pa")
    carried = upstream(slab_summary(moments, tables), tables[6], slab_count)
    wake_kick = slab_kick(moments, carried, tables)
    per_particle = jnp.take(wake_kick, slice_index, axis=1)
    capacity = local_count * 3 // 16
    head_count = moving[0, 0, 0]
    tail_count = moving[0, 0, 1]
    slot_index = lax.broadcasted_iota(jnp.int32, (1, capacity), 1)
    leaving_head = slot_index < head_count
    leaving_tail = slot_index >= capacity - tail_count
    zero_value = jnp.float32(0.0)
    tail_start = local_count - capacity
    moved_all = one_turn(particles, per_particle)
    head_part = moved_all[:, :capacity]
    tail_part = moved_all[:, tail_start:]
    head_send = jnp.where(leaving_head, head_part, zero_value)
    tail_send = jnp.where(leaving_tail, tail_part, zero_value)
    from_behind = from_behind_2(head_send, "gz", -1)
    from_ahead = from_behind_2(tail_send, "gz", 1)
    head_kept = jnp.where(leaving_head, zero_value, head_part)
    tail_kept = jnp.where(leaving_tail, zero_value, tail_part)
    middle_part = moved_all[:, capacity:tail_start]
    particles_out = jnp.concatenate(
        [from_behind, head_kept, middle_part, tail_kept, from_ahead], axis=1
    )
    return (wake_kick, particles_out)


def solution(mesh):
    return jax.shard_map(
        body,
        mesh=mesh,
        in_specs=(P(None, ("gz", "pa")), P(("gz", "pa")), P("gz", "pa", None), P(), P(), P()),
        out_specs=(P(None, "gz"), P(None, ("gz", "pa"))),
        check_vma=False,
    )
```

profile of v0, /device:TPU:16, one launch (start us, length us, event | category | flops | bytes accessed | tf_op | source)
XLA Modules:
  0.0 447.7 jit_solution(7515340950392063301)
XLA Ops:
  2.4 11.5 %scatter_custom_fusion = f32[3,128]{0,1:T(8,128)S(1)} fusion(s32[2048]{0:T(1024)S(1)} %copy-done.1, f32[2048,3]{1,0:T(8,128)S(1)} %copy.80, f32[]{:T(128)} %constant.22.clone.1), kind=kCustom, calls=%fused_computation.37 | custom fusion | flops 6144 | bytes 1540 | tf_op jit(solution)/shard_map/vmap()/scatter-add | solution.py:121
  14.0 99.1 %psum.7 = f32[3,128]{0,1:T(8,128)S(1)} all-reduce(f32[3,128]{0,1:T(8,128)S(1)} %scatter_custom_fusion), channel_id=1, replica_groups=mesh['gz'=16,'pa'=32] {'pa'}, use_global_device_ids=true, to_apply=%region_1.0 | all-reduce | flops 384 | bytes 3072 | tf_op jit(solution)/shard_map/psum | solution.py:184
  113.9 114.3 %while.11 = (s32[]{:T(128)}, f32[2,8,3]{1,0,2:T(2,128)S(1)}, f32[2,8,3]{1,0,2:T(2,128)S(1)}, f32[8]{0:T(128)S(1)}, f32[8]{0:T(128)S(1)}, /*index=5*/s32[]{:T(128)}) while((s32[]{:T(128)}, f32[2,8,3]{1,0,2:T(2,128)S(1)}, f32[2,8,3]{1,0,2:T(2,128)S(1)}, f32[8]{0:T(128)S(1)}, f32[8]{0:T(128)S(1)}, /*index=5*/s32[]{:T(128)}) %tuple.64), condition=%wide.region_5.7_spmd.clone, body=%wide.region_4.6_spmd.clone.sunk | while | flops 242 | bytes 1901 | solution.py:172
  113.9 3.4 collective-permute-start
  117.4 4.2 collective-permute-done
  123.5 5.7 %collective-permute-done = f32[2,8,3]{1,0,2:T(2,128)S(1)} collective-permute-done((f32[2,8,3]{1,0,2:T(2,128)S(1)}, f32[2,8,3]{1,0,2:T(2,128)S(1)}, u32[]{:S(2)}, u32[]{:S(2)}) %collective-permute-start) | collective-permute-done | bytes 224 | tf_op jit(solution)/shard_map/while/body/eval_jaxpr/ppermute | solution.py:25
  131.1 5.7 %collective-permute-done = f32[2,8,3]{1,0,2:T(2,128)S(1)} collective-permute-done((f32[2,8,3]{1,0,2:T(2,128)S(1)}, f32[2,8,3]{1,0,2:T(2,128)S(1)}, u32[]{:S(2)}, u32[]{:S(2)}) %collective-permute-start) | collective-permute-done | bytes 224 | tf_op jit(solution)/shard_map/while/body/eval_jaxpr/ppermute | solution.py:25
  138.7 5.7 %collective-permute-done = f32[2,8,3]{1,0,2:T(2,128)S(1)} collective-permute-done((f32[2,8,3]{1,0,2:T(2,128)S(1)}, f32[2,8,3]{1,0,2:T(2,128)S(1)}, u32[]{:S(2)}, u32[]{:S(2)}) %collective-permute-start) | collective-permute-done | bytes 224 | tf_op jit(solution)/shard_map/while/body/eval_jaxpr/ppermute | solution.py:25
  146.4 5.7 %collective-permute-done = f32[2,8,3]{1,0,2:T(2,128)S(1)} collective-permute-done((f32[2,8,3]{1,0,2:T(2,128)S(1)}, f32[2,8,3]{1,0,2:T(2,128)S(1)}, u32[]{:S(2)}, u32[]{:S(2)}) %collective-permute-start) | collective-permute-done | bytes 224 | tf_op jit(solution)/shard_map/while/body/eval_jaxpr/ppermute | solution.py:25
  154.0 5.7 %collective-permute-done = f32[2,8,3]{1,0,2:T(2,128)S(1)} collective-permute-done((f32[2,8,3]{1,0,2:T(2,128)S(1)}, f32[2,8,3]{1,0,2:T(2,128)S(1)}, u32[]{:S(2)}, u32[]{:S(2)}) %collective-permute-start) | collective-permute-done | bytes 224 | tf_op jit(solution)/shard_map/while/body/eval_jaxpr/ppermute | solution.py:25
  161.6 5.7 %collective-permute-done = f32[2,8,3]{1,0,2:T(2,128)S(1)} collective-permute-done((f32[2,8,3]{1,0,2:T(2,128)S(1)}, f32[2,8,3]{1,0,2:T(2,128)S(1)}, u32[]{:S(2)}, u32[]{:S(2)}) %collective-permute-start) | collective-permute-done | bytes 224 | tf_op jit(solution)/shard_map/while/body/eval_jaxpr/ppermute | solution.py:25
  169.2 5.7 %collective-permute-done = f32[2,8,3]{1,0,2:T(2,128)S(1)} collective-permute-done((f32[2,8,3]{1,0,2:T(2,128)S(1)}, f32[2,8,3]{1,0,2:T(2,128)S(1)}, u32[]{:S(2)}, u32[]{:S(2)}) %collective-permute-start) | collective-permute-done | bytes 224 | tf_op jit(solution)/shard_map/while/body/eval_jaxpr/ppermute | solution.py:25
  176.8 5.7 %collective-permute-done = f32[2,8,3]{1,0,2:T(2,128)S(1)} collective-permute-done((f32[2,8,3]{1,0,2:T(2,128)S(1)}, f32[2,8,3]{1,0,2:T(2,128)S(1)}, u32[]{:S(2)}, u32[]{:S(2)}) %collective-permute-start) | collective-permute-done | bytes 224 | tf_op jit(solution)/shard_map/while/body/eval_jaxpr/ppermute | solution.py:25
  184.5 5.7 %collective-permute-done = f32[2,8,3]{1,0,2:T(2,128)S(1)} collective-permute-done((f32[2,8,3]{1,0,2:T(2,128)S(1)}, f32[2,8,3]{1,0,2:T(2,128)S(1)}, u32[]{:S(2)}, u32[]{:S(2)}) %collective-permute-start) | collective-permute-done | bytes 224 | tf_op jit(solution)/shard_map/while/body/eval_jaxpr/ppermute | solution.py:25
  192.1 5.7 %collective-permute-done = f32[2,8,3]{1,0,2:T(2,128)S(1)} collective-permute-done((f32[2,8,3]{1,0,2:T(2,128)S(1)}, f32[2,8,3]{1,0,2:T(2,128)S(1)}, u32[]{:S(2)}, u32[]{:S(2)}) %collective-permute-start) | collective-permute-done | bytes 224 | tf_op jit(solution)/shard_map/while/body/eval_jaxpr/ppermute | solution.py:25
  199.7 5.7 %collective-permute-done = f32[2,8,3]{1,0,2:T(2,128)S(1)} collective-permute-done((f32[2,8,3]{1,0,2:T(2,128)S(1)}, f32[2,8,3]{1,0,2:T(2,128)S(1)}, u32[]{:S(2)}, u32[]{:S(2)}) %collective-permute-start) | collective-permute-done | bytes 224 | tf_op jit(solution)/shard_map/while/body/eval_jaxpr/ppermute | solution.py:25
  207.3 5.7 %collective-permute-done = f32[2,8,3]{1,0,2:T(2,128)S(1)} collective-permute-done((f32[2,8,3]{1,0,2:T(2,128)S(1)}, f32[2,8,3]{1,0,2:T(2,128)S(1)}, u32[]{:S(2)}, u32[]{:S(2)}) %collective-permute-start) | collective-permute-done | bytes 224 | tf_op jit(solution)/shard_map/while/body/eval_jaxpr/ppermute | solution.py:25
  214.9 5.7 %collective-permute-done = f32[2,8,3]{1,0,2:T(2,128)S(1)} collective-permute-done((f32[2,8,3]{1,0,2:T(2,128)S(1)}, f32[2,8,3]{1,0,2:T(2,128)S(1)}, u32[]{:S(2)}, u32[]{:S(2)}) %collective-permute-start) | collective-permute-done | bytes 224 | tf_op jit(solution)/shard_map/while/body/eval_jaxpr/ppermute | solution.py:25
  222.6 5.7 %collective-permute-done = f32[2,8,3]{1,0,2:T(2,128)S(1)} collective-permute-done((f32[2,8,3]{1,0,2:T(2,128)S(1)}, f32[2,8,3]{1,0,2:T(2,128)S(1)}, u32[]{:S(2)}, u32[]{:S(2)}) %collective-permute-start) | collective-permute-done | bytes 224 | tf_op jit(solution)/shard_map/while/body/eval_jaxpr/ppermute | solution.py:25
  228.4 97.2 %gather_fusion.1 = f32[16384]{0:T(1024)S(1)} fusion(f32[128]{0:T(128)S(1)} %get-tuple-element.75, s32[16384]{0:T(1024)S(1)} %bitcast_clamp_fusion), kind=kCustom, calls=%fused_computation.clone | custom fusion | bytes 196608 | tf_op jit(solution)/shard_map/jit(_take)/gather | solution.py:45
  325.8 97.2 %gather_fusion.2 = f32[16384]{0:T(1024)S(1)} fusion(f32[128]{0:T(128)S(1)} %get-tuple-element.76, s32[16384]{0:T(1024)S(1)} %bitcast_clamp_fusion), kind=kCustom, calls=%fused_computation.1.clone | custom fusion | bytes 196608 | tf_op jit(solution)/shard_map/jit(_take)/gather | solution.py:45
  424.3 5.5 %gather_fusion = f32[2048,3]{1,0:T(8,128)S(1)} fusion(f32[3,128]{0,1:T(8,128)S(1)} %copy.82, s32[2048]{0:T(1024)S(1)} %fusion.32), kind=kCustom, calls=%fused_computation.2 | custom fusion | bytes 57344 | tf_op jit(solution)/shard_map/jit(_take)/gather | solution.py:187
  436.3 3.0 collective-permute-done.1
  441.3 5.8 %collective-permute-done.2 = f32[6,384]{1,0:T(8,128)S(1)} collective-permute-done((f32[6,384]{1,0:T(8,128)S(1)}, f32[6,384]{1,0:T(8,128)S(1)}, u32[]{:S(2)}, u32[]{:S(2)}) %collective-permute-start.2) | collective-permute-done | bytes 9248 | tf_op jit(solution)/shard_map/ppermute | solution.py:25
  (101 shorter events, 39.8 us)
Async XLA Ops:
  1.7 0.7 copy-start.1
  13.9 99.1 %copy-start.2 = (f32[4,8]{1,0:T(4,128)S(1)}, f32[4,8]{1,0:T(4,128)}, u32[]{:S(2)}) copy-start(f32[4,8]{1,0:T(4,128)} %param.15) | copy-start | bytes 388
  13.9 99.1 %copy-start.6 = (f32[8]{0:T(128)S(1)}, f32[8]{0:T(128)}, u32[]{:S(2)}) copy-start(f32[8]{0:T(128)} %param.13) | copy-start | bytes 100
  13.9 99.1 %copy-start.7 = (f32[8]{0:T(128)S(1)}, f32[8]{0:T(128)}, u32[]{:S(2)}) copy-start(f32[8]{0:T(128)} %param.14) | copy-start | bytes 100
  113.9 7.6 %collective-permute-start = (f32[2,8,3]{1,0,2:T(2,128)S(1)}, f32[2,8,3]{1,0,2:T(2,128)S(1)}, u32[]{:S(2)}, u32[]{:S(2)}) collective-permute-start(f32[2,8,3]{1,0,2:T(2,128)S(1)} %maximum_add_fusion.2), channel_id=1, source_target_pairs={{0,32},{32,64},{64,96},{96,128},{128,160},{160,192},{192,224},{224... | collective-permute-start | bytes 584 | tf_op jit(solution)/shard_map/while/body/eval_jaxpr/ppermute | solution.py:25
  121.6 7.6 %collective-permute-start = (f32[2,8,3]{1,0,2:T(2,128)S(1)}, f32[2,8,3]{1,0,2:T(2,128)S(1)}, u32[]{:S(2)}, u32[]{:S(2)}) collective-permute-start(f32[2,8,3]{1,0,2:T(2,128)S(1)} %maximum_add_fusion.2), channel_id=1, source_target_pairs={{0,32},{32,64},{64,96},{96,128},{128,160},{160,192},{192,224},{224... | collective-permute-start | bytes 584 | tf_op jit(solution)/shard_map/while/body/eval_jaxpr/ppermute | solution.py:25
  129.2 7.6 %collective-permute-start = (f32[2,8,3]{1,0,2:T(2,128)S(1)}, f32[2,8,3]{1,0,2:T(2,128)S(1)}, u32[]{:S(2)}, u32[]{:S(2)}) collective-permute-start(f32[2,8,3]{1,0,2:T(2,128)S(1)} %maximum_add_fusion.2), channel_id=1, source_target_pairs={{0,32},{32,64},{64,96},{96,128},{128,160},{160,192},{192,224},{224... | collective-permute-start | bytes 584 | tf_op jit(solution)/shard_map/while/body/eval_jaxpr/ppermute | solution.py:25
  136.8 7.6 %collective-permute-start = (f32[2,8,3]{1,0,2:T(2,128)S(1)}, f32[2,8,3]{1,0,2:T(2,128)S(1)}, u32[]{:S(2)}, u32[]{:S(2)}) collective-permute-start(f32[2,8,3]{1,0,2:T(2,128)S(1)} %maximum_add_fusion.2), channel_id=1, source_target_pairs={{0,32},{32,64},{64,96},{96,128},{128,160},{160,192},{192,224},{224... | collective-permute-start | bytes 584 | tf_op jit(solution)/shard_map/while/body/eval_jaxpr/ppermute | solution.py:25
  144.4 7.6 %collective-permute-start = (f32[2,8,3]{1,0,2:T(2,128)S(1)}, f32[2,8,3]{1,0,2:T(2,128)S(1)}, u32[]{:S(2)}, u32[]{:S(2)}) collective-permute-start(f32[2,8,3]{1,0,2:T(2,128)S(1)} %maximum_add_fusion.2), channel_id=1, source_target_pairs={{0,32},{32,64},{64,96},{96,128},{128,160},{160,192},{192,224},{224... | collective-permute-start | bytes 584 | tf_op jit(solution)/shard_map/while/body/eval_jaxpr/ppermute | solution.py:25
  152.0 7.6 %collective-permute-start = (f32[2,8,3]{1,0,2:T(2,128)S(1)}, f32[2,8,3]{1,0,2:T(2,128)S(1)}, u32[]{:S(2)}, u32[]{:S(2)}) collective-permute-start(f32[2,8,3]{1,0,2:T(2,128)S(1)} %maximum_add_fusion.2), channel_id=1, source_target_pairs={{0,32},{32,64},{64,96},{96,128},{128,160},{160,192},{192,224},{224... | collective-permute-start | bytes 584 | tf_op jit(solution)/shard_map/while/body/eval_jaxpr/ppermute | solution.py:25
  159.7 7.6 %collective-permute-start = (f32[2,8,3]{1,0,2:T(2,128)S(1)}, f32[2,8,3]{1,0,2:T(2,128)S(1)}, u32[]{:S(2)}, u32[]{:S(2)}) collective-permute-start(f32[2,8,3]{1,0,2:T(2,128)S(1)} %maximum_add_fusion.2), channel_id=1, source_target_pairs={{0,32},{32,64},{64,96},{96,128},{128,160},{160,192},{192,224},{224... | collective-permute-start | bytes 584 | tf_op jit(solution)/shard_map/while/body/eval_jaxpr/ppermute | solution.py:25
  167.3 7.6 %collective-permute-start = (f32[2,8,3]{1,0,2:T(2,128)S(1)}, f32[2,8,3]{1,0,2:T(2,128)S(1)}, u32[]{:S(2)}, u32[]{:S(2)}) collective-permute-start(f32[2,8,3]{1,0,2:T(2,128)S(1)} %maximum_add_fusion.2), channel_id=1, source_target_pairs={{0,32},{32,64},{64,96},{96,128},{128,160},{160,192},{192,224},{224... | collective-permute-start | bytes 584 | tf_op jit(solution)/shard_map/while/body/eval_jaxpr/ppermute | solution.py:25
  174.9 7.6 %collective-permute-start = (f32[2,8,3]{1,0,2:T(2,128)S(1)}, f32[2,8,3]{1,0,2:T(2,128)S(1)}, u32[]{:S(2)}, u32[]{:S(2)}) collective-permute-start(f32[2,8,3]{1,0,2:T(2,128)S(1)} %maximum_add_fusion.2), channel_id=1, source_target_pairs={{0,32},{32,64},{64,96},{96,128},{128,160},{160,192},{192,224},{224... | collective-permute-start | bytes 584 | tf_op jit(solution)/shard_map/while/body/eval_jaxpr/ppermute | solution.py:25
  182.5 7.6 %collective-permute-start = (f32[2,8,3]{1,0,2:T(2,128)S(1)}, f32[2,8,3]{1,0,2:T(2,128)S(1)}, u32[]{:S(2)}, u32[]{:S(2)}) collective-permute-start(f32[2,8,3]{1,0,2:T(2,128)S(1)} %maximum_add_fusion.2), channel_id=1, source_target_pairs={{0,32},{32,64},{64,96},{96,128},{128,160},{160,192},{192,224},{224... | collective-permute-start | bytes 584 | tf_op jit(solution)/shard_map/while/body/eval_jaxpr/ppermute | solution.py:25
  190.2 7.6 %collective-permute-start = (f32[2,8,3]{1,0,2:T(2,128)S(1)}, f32[2,8,3]{1,0,2:T(2,128)S(1)}, u32[]{:S(2)}, u32[]{:S(2)}) collective-permute-start(f32[2,8,3]{1,0,2:T(2,128)S(1)} %maximum_add_fusion.2), channel_id=1, source_target_pairs={{0,32},{32,64},{64,96},{96,128},{128,160},{160,192},{192,224},{224... | collective-permute-start | bytes 584 | tf_op jit(solution)/shard_map/while/body/eval_jaxpr/ppermute | solution.py:25
  197.8 7.6 %collective-permute-start = (f32[2,8,3]{1,0,2:T(2,128)S(1)}, f32[2,8,3]{1,0,2:T(2,128)S(1)}, u32[]{:S(2)}, u32[]{:S(2)}) collective-permute-start(f32[2,8,3]{1,0,2:T(2,128)S(1)} %maximum_add_fusion.2), channel_id=1, source_target_pairs={{0,32},{32,64},{64,96},{96,128},{128,160},{160,192},{192,224},{224... | collective-permute-start | bytes 584 | tf_op jit(solution)/shard_map/while/body/eval_jaxpr/ppermute | solution.py:25
  205.4 7.6 %collective-permute-start = (f32[2,8,3]{1,0,2:T(2,128)S(1)}, f32[2,8,3]{1,0,2:T(2,128)S(1)}, u32[]{:S(2)}, u32[]{:S(2)}) collective-permute-start(f32[2,8,3]{1,0,2:T(2,128)S(1)} %maximum_add_fusion.2), channel_id=1, source_target_pairs={{0,32},{32,64},{64,96},{96,128},{128,160},{160,192},{192,224},{224... | collective-permute-start | bytes 584 | tf_op jit(solution)/shard_map/while/body/eval_jaxpr/ppermute | solution.py:25
  213.0 7.6 %collective-permute-start = (f32[2,8,3]{1,0,2:T(2,128)S(1)}, f32[2,8,3]{1,0,2:T(2,128)S(1)}, u32[]{:S(2)}, u32[]{:S(2)}) collective-permute-start(f32[2,8,3]{1,0,2:T(2,128)S(1)} %maximum_add_fusion.2), channel_id=1, source_target_pairs={{0,32},{32,64},{64,96},{96,128},{128,160},{160,192},{192,224},{224... | collective-permute-start | bytes 584 | tf_op jit(solution)/shard_map/while/body/eval_jaxpr/ppermute | solution.py:25
  220.6 7.6 %collective-permute-start = (f32[2,8,3]{1,0,2:T(2,128)S(1)}, f32[2,8,3]{1,0,2:T(2,128)S(1)}, u32[]{:S(2)}, u32[]{:S(2)}) collective-permute-start(f32[2,8,3]{1,0,2:T(2,128)S(1)} %maximum_add_fusion.2), channel_id=1, source_target_pairs={{0,32},{32,64},{64,96},{96,128},{128,160},{160,192},{192,224},{224... | collective-permute-start | bytes 584 | tf_op jit(solution)/shard_map/while/body/eval_jaxpr/ppermute | solution.py:25
  430.1 0.9 copy-start
  431.0 0.7 copy-start.4
  433.7 5.6 %collective-permute-start.1 = (f32[6,384]{1,0:T(8,128)S(1)}, f32[6,384]{1,0:T(8,128)S(1)}, u32[]{:S(2)}, u32[]{:S(2)}) collective-permute-start(f32[6,384]{1,0:T(8,128)S(1)} %slice_select_fusion.1), channel_id=1, source_target_pairs={{32,0},{64,32},{96,64},{128,96},{160,128},{192,160},{224,192},{256... | collective-permute-start | bytes 27656 | tf_op jit(solution)/shard_map/ppermute | solution.py:25
  439.4 7.7 %collective-permute-start.2 = (f32[6,384]{1,0:T(8,128)S(1)}, f32[6,384]{1,0:T(8,128)S(1)}, u32[]{:S(2)}, u32[]{:S(2)}) collective-permute-start(f32[6,384]{1,0:T(8,128)S(1)} %get-tuple-element.109), channel_id=1, source_target_pairs={{0,32},{32,64},{64,96},{96,128},{128,160},{160,192},{192,224},{224... | collective-permute-start | bytes 27656 | tf_op jit(solution)/shard_map/ppermute | solution.py:25
  447.1 0.6 copy-start.5
  (1 other events, 0.6 us)
where the time goes:
time: 450 us; the launch traced here: 448 us
  local copies, waits for them, and re-layouts  204 us (45%)
  blocking collectives  99.1 us (22%)
  waiting for transfers between devices  92.3 us (21%)
  starting transfers between devices  34.1 us (8%)
  other arithmetic  15 us (3%)
    gather x2, local copies, waits for them, and re-layouts, toeplitz(): picked = jnp.take(wave, jnp.clip(offset, 0, slab_width - 1))  194 us
    psum x1, blocking collectives, body(): moments = lax.psum(partial_moments, 'pa')  99.1 us
    ppermute x17, waiting for transfers between devices, from_behind_2(): lax.ppermute(value, axis, [(source, source + steps) for source in range(l...  92.3 us
    ppermute x17, starting transfers between devices, from_behind_2(): lax.ppermute(value, axis, [(source, source + steps) for source in range(l...  34.1 us
    scatter-add x1, other arithmetic, deposit(): jax.ops.segment_sum(column, index, num_segments=segments)  11.5 us
  transfers between devices with their start and end apart: 17, of which 17 were waited for; matrix products, arithmetic and copies ran while one was open for 0% of the time, Pallas kernels for 0%

commit v1 on v0

--- a/solution.py
+++ b/solution.py
@@ -181,7 +181,9 @@
     mean_fill = local_count * member_count / slab_width
     values = moment_values(particles, mean_fill)
     partial_moments = deposit(values, slice_index, slab_width)
-    moments = lax.psum(partial_moments, "pa")
+    moments = partial_moments
+    for hop in (1, 2, 4, 8, 16):
+        moments = moments + lax.ppermute(moments, "pa", [(dev, dev ^ hop) for dev in range(32)])
     carried = upstream(slab_summary(moments, tables), tables[6], slab_count)
     wake_kick = slab_kick(moments, carried, tables)
     per_particle = jnp.take(wake_kick, slice_index, axis=1)

time: 450 us -> 396 us (0.88)
  blocking collectives: 99.1 us -> 0 us
  starting transfers between devices: 34.1 us -> 66.7 us
  waiting for transfers between devices: 92.3 us -> 104 us
    psum x1 -> x0, blocking collectives: 99.1 us -> none  [body(): moments = lax.psum(partial_moments, 'pa')]
    ppermute x0 -> x5, starting transfers between devices: none -> 32.6 us  [body(): lax.ppermute(moments, 'pa', [(dev, dev ^ hop) for dev in range(32)])]
    ppermute x0 -> x5, waiting for transfers between devices: none -> 10.9 us  [body(): lax.ppermute(moments, 'pa', [(dev, dev ^ hop) for dev in range(32)])]
  transfers between devices with their start and end apart: 17 -> 22, of which waited for: 17 -> 20; matrix products, arithmetic and copies ran while one was open for 0% -> 50% of each run, Pallas kernels for 0% -> 0%
where the time goes in v1:
time: 396 us; the launch traced here: 394 us
  local copies, waits for them, and re-layouts  205 us (52%)
  waiting for transfers between devices  104 us (26%)
  starting transfers between devices  66.7 us (17%)
  other arithmetic  15 us (4%)
    gather x2, local copies, waits for them, and re-layouts, toeplitz(): picked = jnp.take(wave, jnp.clip(offset, 0, slab_width - 1))  194 us
    ppermute x17, waiting for transfers between devices, from_behind_2(): lax.ppermute(value, axis, [(source, source + steps) for source in range(l...  92.9 us
    ppermute x17, starting transfers between devices, from_behind_2(): lax.ppermute(value, axis, [(source, source + steps) for source in range(l...  34.1 us
    ppermute x5, starting transfers between devices, body(): lax.ppermute(moments, 'pa', [(dev, dev ^ hop) for dev in range(32)])  32.6 us
    scatter-add x1, other arithmetic, deposit(): jax.ops.segment_sum(column, index, num_segments=segments)  11.5 us
    ppermute x5, waiting for transfers between devices, body(): lax.ppermute(moments, 'pa', [(dev, dev ^ hop) for dev in range(32)])  10.9 us
  transfers between devices with their start and end apart: 22, of which 20 were waited for; matrix products, arithmetic and copies ran while one was open for 50% of the time, Pallas kernels for 0%

profile of v1, /device:TPU:16, one launch (start us, length us, event | category | flops | bytes accessed | tf_op | source)
XLA Modules:
  0.0 394.0 jit_solution(1549594771581674540)
XLA Ops:
  2.4 11.5 %scatter_custom_fusion = f32[3,128]{0,1:T(8,128)S(1)} fusion(s32[2048]{0:T(1024)S(1)} %copy-done.1, f32[2048,3]{1,0:T(8,128)S(1)} %copy.80, f32[]{:T(128)} %constant.22.clone.1), kind=kCustom, calls=%fused_computation.36 | custom fusion | flops 6144 | bytes 1540 | tf_op jit(solution)/shard_map/vmap()/scatter-add | solution.py:121
  23.9 5.2 %collective-permute-start.3 = (f32[3,128]{0,1:T(8,128)S(1)}, f32[3,128]{0,1:T(8,128)S(1)}, u32[]{:S(2)}, u32[]{:S(2)}) collective-permute-start(f32[3,128]{0,1:T(8,128)S(1)} %add.153), channel_id=1, source_target_pairs={{0,4},{1,5},{2,6},{3,7},{4,0},{5,1},{6,2},{7,3},{8,12},{9,13},{10,... | collective-permute-start | bytes 4616 | tf_op jit(solution)/shard_map/ppermute | solution.py:186
  32.8 9.1 %collective-permute-start.4 = (f32[3,128]{0,1:T(8,128)S(1)}, f32[3,128]{0,1:T(8,128)S(1)}, u32[]{:S(2)}, u32[]{:S(2)}) collective-permute-start(f32[3,128]{0,1:T(8,128)S(1)} %add.154), channel_id=1, source_target_pairs={{0,8},{1,9},{2,10},{3,11},{4,12},{5,13},{6,14},{7,15},{8,0},{9,1},... | collective-permute-start | bytes 4616 | tf_op jit(solution)/shard_map/ppermute | solution.py:186
  41.9 5.2 %collective-permute-done.4 = f32[3,128]{0,1:T(8,128)S(1)} collective-permute-done((f32[3,128]{0,1:T(8,128)S(1)}, f32[3,128]{0,1:T(8,128)S(1)}, u32[]{:S(2)}, u32[]{:S(2)}) %collective-permute-start.4) | collective-permute-done | bytes 1568 | tf_op jit(solution)/shard_map/ppermute | solution.py:186
  47.1 12.6 %collective-permute-start.5 = (f32[3,128]{0,1:T(8,128)S(1)}, f32[3,128]{0,1:T(8,128)S(1)}, u32[]{:S(2)}, u32[]{:S(2)}) collective-permute-start(f32[3,128]{0,1:T(8,128)S(1)} %add.155), channel_id=1, source_target_pairs={{0,16},{1,17},{2,18},{3,19},{4,20},{5,21},{6,22},{7,23},{8,24},{9,... | collective-permute-start | bytes 4616 | tf_op jit(solution)/shard_map/ppermute | solution.py:186
  60.3 97.2 %gather_fusion.1 = f32[16384]{0:T(1024)S(1)} fusion(f32[128]{0:T(128)S(1)} %get-tuple-element.75, s32[16384]{0:T(1024)S(1)} %bitcast_clamp_fusion), kind=kCustom, calls=%fused_computation.clone | custom fusion | bytes 196608 | tf_op jit(solution)/shard_map/jit(_take)/gather | solution.py:45
  157.6 97.2 %gather_fusion.2 = f32[16384]{0:T(1024)S(1)} fusion(f32[128]{0:T(128)S(1)} %get-tuple-element.76, s32[16384]{0:T(1024)S(1)} %bitcast_clamp_fusion), kind=kCustom, calls=%fused_computation.1.clone | custom fusion | bytes 196608 | tf_op jit(solution)/shard_map/jit(_take)/gather | solution.py:45
  256.2 114.3 %while.11 = (s32[]{:T(128)}, f32[2,8,3]{1,0,2:T(2,128)S(1)}, f32[2,8,3]{1,0,2:T(2,128)S(1)}, f32[8]{0:T(128)S(1)}, f32[8]{0:T(128)S(1)}, /*index=5*/s32[]{:T(128)}) while((s32[]{:T(128)}, f32[2,8,3]{1,0,2:T(2,128)S(1)}, f32[2,8,3]{1,0,2:T(2,128)S(1)}, f32[8]{0:T(128)S(1)}, f32[8]{0:T(128)S(1)}, /*index=5*/s32[]{:T(128)}) %tuple.64), condition=%wide.region_4.6_spmd.clone, body=%wide.region_3.5_spmd.clone.sunk | while | flops 242 | bytes 1901 | solution.py:172
  265.8 5.7 %collective-permute-done = f32[2,8,3]{1,0,2:T(2,128)S(1)} collective-permute-done((f32[2,8,3]{1,0,2:T(2,128)S(1)}, f32[2,8,3]{1,0,2:T(2,128)S(1)}, u32[]{:S(2)}, u32[]{:S(2)}) %collective-permute-start) | collective-permute-done | bytes 224 | tf_op jit(solution)/shard_map/while/body/eval_jaxpr/ppermute | solution.py:25
  273.4 5.7 %collective-permute-done = f32[2,8,3]{1,0,2:T(2,128)S(1)} collective-permute-done((f32[2,8,3]{1,0,2:T(2,128)S(1)}, f32[2,8,3]{1,0,2:T(2,128)S(1)}, u32[]{:S(2)}, u32[]{:S(2)}) %collective-permute-start) | collective-permute-done | bytes 224 | tf_op jit(solution)/shard_map/while/body/eval_jaxpr/ppermute | solution.py:25
  281.0 5.7 %collective-permute-done = f32[2,8,3]{1,0,2:T(2,128)S(1)} collective-permute-done((f32[2,8,3]{1,0,2:T(2,128)S(1)}, f32[2,8,3]{1,0,2:T(2,128)S(1)}, u32[]{:S(2)}, u32[]{:S(2)}) %collective-permute-start) | collective-permute-done | bytes 224 | tf_op jit(solution)/shard_map/while/body/eval_jaxpr/ppermute | solution.py:25
  288.7 5.7 %collective-permute-done = f32[2,8,3]{1,0,2:T(2,128)S(1)} collective-permute-done((f32[2,8,3]{1,0,2:T(2,128)S(1)}, f32[2,8,3]{1,0,2:T(2,128)S(1)}, u32[]{:S(2)}, u32[]{:S(2)}) %collective-permute-start) | collective-permute-done | bytes 224 | tf_op jit(solution)/shard_map/while/body/eval_jaxpr/ppermute | solution.py:25
  296.3 5.7 %collective-permute-done = f32[2,8,3]{1,0,2:T(2,128)S(1)} collective-permute-done((f32[2,8,3]{1,0,2:T(2,128)S(1)}, f32[2,8,3]{1,0,2:T(2,128)S(1)}, u32[]{:S(2)}, u32[]{:S(2)}) %collective-permute-start) | collective-permute-done | bytes 224 | tf_op jit(solution)/shard_map/while/body/eval_jaxpr/ppermute | solution.py:25
  303.9 5.7 %collective-permute-done = f32[2,8,3]{1,0,2:T(2,128)S(1)} collective-permute-done((f32[2,8,3]{1,0,2:T(2,128)S(1)}, f32[2,8,3]{1,0,2:T(2,128)S(1)}, u32[]{:S(2)}, u32[]{:S(2)}) %collective-permute-start) | collective-permute-done | bytes 224 | tf_op jit(solution)/shard_map/while/body/eval_jaxpr/ppermute | solution.py:25
  311.5 5.7 %collective-permute-done = f32[2,8,3]{1,0,2:T(2,128)S(1)} collective-permute-done((f32[2,8,3]{1,0,2:T(2,128)S(1)}, f32[2,8,3]{1,0,2:T(2,128)S(1)}, u32[]{:S(2)}, u32[]{:S(2)}) %collective-permute-start) | collective-permute-done | bytes 224 | tf_op jit(solution)/shard_map/while/body/eval_jaxpr/ppermute | solution.py:25
  319.1 5.7 %collective-permute-done = f32[2,8,3]{1,0,2:T(2,128)S(1)} collective-permute-done((f32[2,8,3]{1,0,2:T(2,128)S(1)}, f32[2,8,3]{1,0,2:T(2,128)S(1)}, u32[]{:S(2)}, u32[]{:S(2)}) %collective-permute-start) | collective-permute-done | bytes 224 | tf_op jit(solution)/shard_map/while/body/eval_jaxpr/ppermute | solution.py:25
  326.8 5.7 %collective-permute-done = f32[2,8,3]{1,0,2:T(2,128)S(1)} collective-permute-done((f32[2,8,3]{1,0,2:T(2,128)S(1)}, f32[2,8,3]{1,0,2:T(2,128)S(1)}, u32[]{:S(2)}, u32[]{:S(2)}) %collective-permute-start) | collective-permute-done | bytes 224 | tf_op jit(solution)/shard_map/while/body/eval_jaxpr/ppermute | solution.py:25
  334.4 5.7 %collective-permute-done = f32[2,8,3]{1,0,2:T(2,128)S(1)} collective-permute-done((f32[2,8,3]{1,0,2:T(2,128)S(1)}, f32[2,8,3]{1,0,2:T(2,128)S(1)}, u32[]{:S(2)}, u32[]{:S(2)}) %collective-permute-start) | collective-permute-done | bytes 224 | tf_op jit(solution)/shard_map/while/body/eval_jaxpr/ppermute | solution.py:25
  342.0 5.7 %collective-permute-done = f32[2,8,3]{1,0,2:T(2,128)S(1)} collective-permute-done((f32[2,8,3]{1,0,2:T(2,128)S(1)}, f32[2,8,3]{1,0,2:T(2,128)S(1)}, u32[]{:S(2)}, u32[]{:S(2)}) %collective-permute-start) | collective-permute-done | bytes 224 | tf_op jit(solution)/shard_map/while/body/eval_jaxpr/ppermute | solution.py:25
  349.6 5.7 %collective-permute-done = f32[2,8,3]{1,0,2:T(2,128)S(1)} collective-permute-done((f32[2,8,3]{1,0,2:T(2,128)S(1)}, f32[2,8,3]{1,0,2:T(2,128)S(1)}, u32[]{:S(2)}, u32[]{:S(2)}) %collective-permute-start) | collective-permute-done | bytes 224 | tf_op jit(solution)/shard_map/while/body/eval_jaxpr/ppermute | solution.py:25
  357.2 5.7 %collective-permute-done = f32[2,8,3]{1,0,2:T(2,128)S(1)} collective-permute-done((f32[2,8,3]{1,0,2:T(2,128)S(1)}, f32[2,8,3]{1,0,2:T(2,128)S(1)}, u32[]{:S(2)}, u32[]{:S(2)}) %collective-permute-start) | collective-permute-done | bytes 224 | tf_op jit(solution)/shard_map/while/body/eval_jaxpr/ppermute | solution.py:25
  364.9 5.7 %collective-permute-done = f32[2,8,3]{1,0,2:T(2,128)S(1)} collective-permute-done((f32[2,8,3]{1,0,2:T(2,128)S(1)}, f32[2,8,3]{1,0,2:T(2,128)S(1)}, u32[]{:S(2)}, u32[]{:S(2)}) %collective-permute-start) | collective-permute-done | bytes 224 | tf_op jit(solution)/shard_map/while/body/eval_jaxpr/ppermute | solution.py:25
  372.1 5.5 %gather_fusion = f32[2048,3]{1,0:T(8,128)S(1)} fusion(f32[3,128]{0,1:T(8,128)S(1)} %copy.82, s32[2048]{0:T(1024)S(1)} %fusion.31), kind=kCustom, calls=%fused_computation.2 | custom fusion | bytes 57344 | tf_op jit(solution)/shard_map/jit(_take)/gather | solution.py:189
  387.6 5.8 %collective-permute-done.7 = f32[6,384]{1,0:T(8,128)S(1)} collective-permute-done((f32[6,384]{1,0:T(8,128)S(1)}, f32[6,384]{1,0:T(8,128)S(1)}, u32[]{:S(2)}, u32[]{:S(2)}) %collective-permute-start.7) | collective-permute-done | bytes 9248 | tf_op jit(solution)/shard_map/ppermute | solution.py:25
  (115 shorter events, 63.7 us)
Async XLA Ops:
  13.9 3.4 collective-permute-start.1
  17.3 6.6 %collective-permute-start.2 = (f32[3,128]{0,1:T(8,128)S(1)}, f32[3,128]{0,1:T(8,128)S(1)}, u32[]{:S(2)}, u32[]{:S(2)}) collective-permute-start(f32[3,128]{0,1:T(8,128)S(1)} %add.152), channel_id=1, source_target_pairs={{0,2},{1,3},{2,0},{3,1},{4,6},{5,7},{6,4},{7,5},{8,10},{9,11},{10,... | collective-permute-start | bytes 4616 | tf_op jit(solution)/shard_map/ppermute | solution.py:186
  21.3 7.8 %copy-start.4 = (s32[1,1,2]{2,1,0:T(1,128)S(1)}, s32[1,1,2]{2,1,0:T(1,128)}, u32[]{:S(2)}) copy-start(s32[1,1,2]{2,1,0:T(1,128)} %param.12) | copy-start | bytes 28
  23.9 8.8 %collective-permute-start.3 = (f32[3,128]{0,1:T(8,128)S(1)}, f32[3,128]{0,1:T(8,128)S(1)}, u32[]{:S(2)}, u32[]{:S(2)}) collective-permute-start(f32[3,128]{0,1:T(8,128)S(1)} %add.153), channel_id=1, source_target_pairs={{0,4},{1,5},{2,6},{3,7},{4,0},{5,1},{6,2},{7,3},{8,12},{9,13},{10,... | collective-permute-start | bytes 4616 | tf_op jit(solution)/shard_map/ppermute | solution.py:186
  32.8 14.3 %collective-permute-start.4 = (f32[3,128]{0,1:T(8,128)S(1)}, f32[3,128]{0,1:T(8,128)S(1)}, u32[]{:S(2)}, u32[]{:S(2)}) collective-permute-start(f32[3,128]{0,1:T(8,128)S(1)} %add.154), channel_id=1, source_target_pairs={{0,8},{1,9},{2,10},{3,11},{4,12},{5,13},{6,14},{7,15},{8,0},{9,1},... | collective-permute-start | bytes 4616 | tf_op jit(solution)/shard_map/ppermute | solution.py:186
  47.1 208.3 %collective-permute-start.5 = (f32[3,128]{0,1:T(8,128)S(1)}, f32[3,128]{0,1:T(8,128)S(1)}, u32[]{:S(2)}, u32[]{:S(2)}) collective-permute-start(f32[3,128]{0,1:T(8,128)S(1)} %add.155), channel_id=1, source_target_pairs={{0,16},{1,17},{2,18},{3,19},{4,20},{5,21},{6,22},{7,23},{8,24},{9,... | collective-permute-start | bytes 4616 | tf_op jit(solution)/shard_map/ppermute | solution.py:186
  256.3 7.6 %collective-permute-start = (f32[2,8,3]{1,0,2:T(2,128)S(1)}, f32[2,8,3]{1,0,2:T(2,128)S(1)}, u32[]{:S(2)}, u32[]{:S(2)}) collective-permute-start(f32[2,8,3]{1,0,2:T(2,128)S(1)} %maximum_add_fusion.3), channel_id=1, source_target_pairs={{0,32},{32,64},{64,96},{96,128},{128,160},{160,192},{192,224},{224... | collective-permute-start | bytes 584 | tf_op jit(solution)/shard_map/while/body/eval_jaxpr/ppermute | solution.py:25
  263.9 7.6 %collective-permute-start = (f32[2,8,3]{1,0,2:T(2,128)S(1)}, f32[2,8,3]{1,0,2:T(2,128)S(1)}, u32[]{:S(2)}, u32[]{:S(2)}) collective-permute-start(f32[2,8,3]{1,0,2:T(2,128)S(1)} %maximum_add_fusion.3), channel_id=1, source_target_pairs={{0,32},{32,64},{64,96},{96,128},{128,160},{160,192},{192,224},{224... | collective-permute-start | bytes 584 | tf_op jit(solution)/shard_map/while/body/eval_jaxpr/ppermute | solution.py:25
  271.5 7.6 %collective-permute-start = (f32[2,8,3]{1,0,2:T(2,128)S(1)}, f32[2,8,3]{1,0,2:T(2,128)S(1)}, u32[]{:S(2)}, u32[]{:S(2)}) collective-permute-start(f32[2,8,3]{1,0,2:T(2,128)S(1)} %maximum_add_fusion.3), channel_id=1, source_target_pairs={{0,32},{32,64},{64,96},{96,128},{128,160},{160,192},{192,224},{224... | collective-permute-start | bytes 584 | tf_op jit(solution)/shard_map/while/body/eval_jaxpr/ppermute | solution.py:25
  279.1 7.6 %collective-permute-start = (f32[2,8,3]{1,0,2:T(2,128)S(1)}, f32[2,8,3]{1,0,2:T(2,128)S(1)}, u32[]{:S(2)}, u32[]{:S(2)}) collective-permute-start(f32[2,8,3]{1,0,2:T(2,128)S(1)} %maximum_add_fusion.3), channel_id=1, source_target_pairs={{0,32},{32,64},{64,96},{96,128},{128,160},{160,192},{192,224},{224... | collective-permute-start | bytes 584 | tf_op jit(solution)/shard_map/while/body/eval_jaxpr/ppermute | solution.py:25
  286.7 7.6 %collective-permute-start = (f32[2,8,3]{1,0,2:T(2,128)S(1)}, f32[2,8,3]{1,0,2:T(2,128)S(1)}, u32[]{:S(2)}, u32[]{:S(2)}) collective-permute-start(f32[2,8,3]{1,0,2:T(2,128)S(1)} %maximum_add_fusion.3), channel_id=1, source_target_pairs={{0,32},{32,64},{64,96},{96,128},{128,160},{160,192},{192,224},{224... | collective-permute-start | bytes 584 | tf_op jit(solution)/shard_map/while/body/eval_jaxpr/ppermute | solution.py:25
  294.4 7.6 %collective-permute-start = (f32[2,8,3]{1,0,2:T(2,128)S(1)}, f32[2,8,3]{1,0,2:T(2,128)S(1)}, u32[]{:S(2)}, u32[]{:S(2)}) collective-permute-start(f32[2,8,3]{1,0,2:T(2,128)S(1)} %maximum_add_fusion.3), channel_id=1, source_target_pairs={{0,32},{32,64},{64,96},{96,128},{128,160},{160,192},{192,224},{224... | collective-permute-start | bytes 584 | tf_op jit(solution)/shard_map/while/body/eval_jaxpr/ppermute | solution.py:25
  302.0 7.6 %collective-permute-start = (f32[2,8,3]{1,0,2:T(2,128)S(1)}, f32[2,8,3]{1,0,2:T(2,128)S(1)}, u32[]{:S(2)}, u32[]{:S(2)}) collective-permute-start(f32[2,8,3]{1,0,2:T(2,128)S(1)} %maximum_add_fusion.3), channel_id=1, source_target_pairs={{0,32},{32,64},{64,96},{96,128},{128,160},{160,192},{192,224},{224... | collective-permute-start | bytes 584 | tf_op jit(solution)/shard_map/while/body/eval_jaxpr/ppermute | solution.py:25
  309.6 7.6 %collective-permute-start = (f32[2,8,3]{1,0,2:T(2,128)S(1)}, f32[2,8,3]{1,0,2:T(2,128)S(1)}, u32[]{:S(2)}, u32[]{:S(2)}) collective-permute-start(f32[2,8,3]{1,0,2:T(2,128)S(1)} %maximum_add_fusion.3), channel_id=1, source_target_pairs={{0,32},{32,64},{64,96},{96,128},{128,160},{160,192},{192,224},{224... | collective-permute-start | bytes 584 | tf_op jit(solution)/shard_map/while/body/eval_jaxpr/ppermute | solution.py:25
  317.2 7.6 %collective-permute-start = (f32[2,8,3]{1,0,2:T(2,128)S(1)}, f32[2,8,3]{1,0,2:T(2,128)S(1)}, u32[]{:S(2)}, u32[]{:S(2)}) collective-permute-start(f32[2,8,3]{1,0,2:T(2,128)S(1)} %maximum_add_fusion.3), channel_id=1, source_target_pairs={{0,32},{32,64},{64,96},{96,128},{128,160},{160,192},{192,224},{224... | collective-permute-start | bytes 584 | tf_op jit(solution)/shard_map/while/body/eval_jaxpr/ppermute | solution.py:25
  324.8 7.6 %collective-permute-start = (f32[2,8,3]{1,0,2:T(2,128)S(1)}, f32[2,8,3]{1,0,2:T(2,128)S(1)}, u32[]{:S(2)}, u32[]{:S(2)}) collective-permute-start(f32[2,8,3]{1,0,2:T(2,128)S(1)} %maximum_add_fusion.3), channel_id=1, source_target_pairs={{0,32},{32,64},{64,96},{96,128},{128,160},{160,192},{192,224},{224... | collective-permute-start | bytes 584 | tf_op jit(solution)/shard_map/while/body/eval_jaxpr/ppermute | solution.py:25
  332.5 7.6 %collective-permute-start = (f32[2,8,3]{1,0,2:T(2,128)S(1)}, f32[2,8,3]{1,0,2:T(2,128)S(1)}, u32[]{:S(2)}, u32[]{:S(2)}) collective-permute-start(f32[2,8,3]{1,0,2:T(2,128)S(1)} %maximum_add_fusion.3), channel_id=1, source_target_pairs={{0,32},{32,64},{64,96},{96,128},{128,160},{160,192},{192,224},{224... | collective-permute-start | bytes 584 | tf_op jit(solution)/shard_map/while/body/eval_jaxpr/ppermute | solution.py:25
  340.1 7.6 %collective-permute-start = (f32[2,8,3]{1,0,2:T(2,128)S(1)}, f32[2,8,3]{1,0,2:T(2,128)S(1)}, u32[]{:S(2)}, u32[]{:S(2)}) collective-permute-start(f32[2,8,3]{1,0,2:T(2,128)S(1)} %maximum_add_fusion.3), channel_id=1, source_target_pairs={{0,32},{32,64},{64,96},{96,128},{128,160},{160,192},{192,224},{224... | collective-permute-start | bytes 584 | tf_op jit(solution)/shard_map/while/body/eval_jaxpr/ppermute | solution.py:25
  347.7 7.6 %collective-permute-start = (f32[2,8,3]{1,0,2:T(2,128)S(1)}, f32[2,8,3]{1,0,2:T(2,128)S(1)}, u32[]{:S(2)}, u32[]{:S(2)}) collective-permute-start(f32[2,8,3]{1,0,2:T(2,128)S(1)} %maximum_add_fusion.3), channel_id=1, source_target_pairs={{0,32},{32,64},{64,96},{96,128},{128,160},{160,192},{192,224},{224... | collective-permute-start | bytes 584 | tf_op jit(solution)/shard_map/while/body/eval_jaxpr/ppermute | solution.py:25
  355.3 7.6 %collective-permute-start = (f32[2,8,3]{1,0,2:T(2,128)S(1)}, f32[2,8,3]{1,0,2:T(2,128)S(1)}, u32[]{:S(2)}, u32[]{:S(2)}) collective-permute-start(f32[2,8,3]{1,0,2:T(2,128)S(1)} %maximum_add_fusion.3), channel_id=1, source_target_pairs={{0,32},{32,64},{64,96},{96,128},{128,160},{160,192},{192,224},{224... | collective-permute-start | bytes 584 | tf_op jit(solution)/shard_map/while/body/eval_jaxpr/ppermute | solution.py:25
  362.9 7.6 %collective-permute-start = (f32[2,8,3]{1,0,2:T(2,128)S(1)}, f32[2,8,3]{1,0,2:T(2,128)S(1)}, u32[]{:S(2)}, u32[]{:S(2)}) collective-permute-start(f32[2,8,3]{1,0,2:T(2,128)S(1)} %maximum_add_fusion.3), channel_id=1, source_target_pairs={{0,32},{32,64},{64,96},{96,128},{128,160},{160,192},{192,224},{224... | collective-permute-start | bytes 584 | tf_op jit(solution)/shard_map/while/body/eval_jaxpr/ppermute | solution.py:25
  377.9 0.9 copy-start
  380.1 5.6 %collective-permute-start.6 = (f32[6,384]{1,0:T(8,128)S(1)}, f32[6,384]{1,0:T(8,128)S(1)}, u32[]{:S(2)}, u32[]{:S(2)}) collective-permute-start(f32[6,384]{1,0:T(8,128)S(1)} %slice_select_fusion.1), channel_id=1, source_target_pairs={{32,0},{64,32},{96,64},{128,96},{160,128},{192,160},{224,192},{256... | collective-permute-start | bytes 27656 | tf_op jit(solution)/shard_map/ppermute | solution.py:25
  385.7 7.7 %collective-permute-start.7 = (f32[6,384]{1,0:T(8,128)S(1)}, f32[6,384]{1,0:T(8,128)S(1)}, u32[]{:S(2)}, u32[]{:S(2)}) collective-permute-start(f32[6,384]{1,0:T(8,128)S(1)} %get-tuple-element.109), channel_id=1, source_target_pairs={{0,32},{32,64},{64,96},{96,128},{128,160},{160,192},{192,224},{224... | collective-permute-start | bytes 27656 | tf_op jit(solution)/shard_map/ppermute | solution.py:25
  (6 other events, 3.9 us)
